TPU v7x, 32 devices: a whole 2x2x4 slice. The times are simulated.
32 devices in a mesh: dp: 16 (over z, y, core), shard: 2 (over x).
Axes of the slice: x: 2, y: 2, z: 4, core: 2. Of those that a mesh axis runs over, the one named last changes fastest.
Arguments:
- fast_weights: float32 [16, 1280, 3072], P('dp', None, 'shard'), may hold values from -6 to 6
- gradient: bfloat16 [16, 1280, 3072], P('dp', None, 'shard'), may hold values from -6 to 6
- first_moment: float32 [16, 1280, 3072], P('dp', None, 'shard'), may hold values from -0.6 to 0.6
- second_moment: float32 [16, 1280, 3072], P('dp', None, 'shard'), may hold values from 0.0001 to 1
- slow_weights: float32 [1280, 3072], P('dp', 'shard'), may hold values from -6 to 6
Outputs:
- fresh_weights: float32 [1280, 3072], P(None, 'shard')
- slow_synced: float32 [1280, 3072], P('dp', 'shard')
- new_first: float32 [16, 1280, 3072], P('dp', None, 'shard')
- new_second: float32 [16, 1280, 3072], P('dp', None, 'shard')
All inputs are finite; a program needn't handle non-finite values.
Results may differ from a plain program's by a relative error of at most 0.0003.
Values sent between devices are 32-bit elements; how exact they have to be, the bound alone decides.
A program may use at most 128 MiB of HBM per device.

v0:
```python
import jax
import jax.numpy as jnp
from jax import lax
from jax.sharding import PartitionSpec as P

beta_first = 0.9
beta_second = 0.999
learning_rate = 0.01
weight_decay = 0.05
epsilon = 1e-08
blend_rate = 0.5
first_bias = 1.0 - 0.9**5
second_bias = 1.0 - 0.999**5


def local(fast_weights, gradient, first_moment, second_moment, slow_weights):
    grad_value = gradient.astype(jnp.float32)
    new_first = beta_first * first_moment + (1.0 - beta_first) * grad_value
    new_second = beta_second * second_moment + (1.0 - beta_second) * grad_value * grad_value
    direction = new_first / first_bias / (jnp.sqrt(new_second / second_bias) + epsilon)
    stepped = fast_weights - learning_rate * (direction + weight_decay * fast_weights)
    groups = lax.axis_size("dp")
    summed = lax.psum_scatter(stepped[0], "dp", scatter_dimension=0, tiled=True)
    average = summed / groups
    slow_synced = slow_weights + blend_rate * (average - slow_weights)
    fresh_weights = lax.all_gather(slow_synced, "dp", axis=0, tiled=True)
    return (fresh_weights, slow_synced, new_first, new_second)


def solution(mesh):
    return jax.shard_map(
        local,
        mesh=mesh,
        in_specs=(
            P("dp", None, "shard"),
            P("dp", None, "shard"),
            P("dp", None, "shard"),
            P("dp", None, "shard"),
            P("dp", "shard"),
        ),
        out_specs=(
            P(None, "shard"),
            P("dp", "shard"),
            P("dp", None, "shard"),
            P("dp", None, "shard"),
        ),
        check_vma=False,
    )
```

profile of v0, /device:TPU:0, one launch (start us, length us, event | category | flops | bytes accessed | tf_op | source)
XLA Modules:
  0.0 212.0 jit_solution(17143906393350206255)
XLA Ops:
  7.2 0.0 reduce-scatter.2.cloned.1.call-start
  7.2 19.3 %subtract_bitcast_fusion = (f32[1280,1536]{1,0:T(8,128)}, f32[1,1280,1536]{2,1,0:T(8,128)}, f32[1,1280,1536]{2,1,0:T(8,128)}) fusion(f32[1,1280,1536]{2,1,0:T(8,128)} %param.5, bf16[1,1280,1536]{2,1,0:T(8,128)(2,1)} %param.6, f32[1,1280,1536]{2,1,0:T(8,128)} %param.7, f32[1,1280,1536]{2,1,0:T(8,128)} %param.8), kind=kLoop, calls=%fused_computation.4 | loop fusion | flops 31457280 | bytes 51118080 | tf_op jit(solution)/shard_map/squeeze | solution.py:23
  26.5 0.0 copy-start
  26.5 0.0 reduce-scatter.2.cloned.1.call-update
  26.5 0.0 all-gather.2.cloned.1.call-start
  26.6 98.0 %reduce-scatter.2.cloned.1.call-done = f32[80,1536]{1,0:T(8,128)} async-done(((f32[1280,1536]{1,0:T(8,128)}), f32[80,1536]{1,0:T(8,128)}) %reduce-scatter.2.cloned.1.call-update) | async-done | bytes 491536 | tf_op jit(solution)/shard_map/reduce_scatter | solution.py:23
  124.5 0.0 copy-done
  124.6 1.9 multiply_add_fusion
  126.4 0.0 all-gather.2.cloned.1.call-update
  126.5 71.6 %all-gather.2.cloned.1.call-done = f32[1280,1536]{1,0:T(8,128)} async-done(((f32[80,1536]{1,0:T(8,128)}), f32[1280,1536]{1,0:T(8,128)}) %all-gather.2.cloned.1.call-update) | async-done | bytes 7864336 | tf_op jit(solution)/shard_map/all_gather | solution.py:26
  198.1 7.1 %copy.10 = f32[1280,1536]{1,0:T(8,128)} copy(f32[1280,1536]{1,0:T(8,128)} %all-gather.2.cloned.1.call-done) | data formatting | bytes 15728640
Async XLA Ops:
  7.2 117.4 %reduce-scatter.2.cloned.1.call-start = ((), (), s32[]{:S(2)}) async-start(), calls=%async_computation.1 | async-start | bytes 8355840 | tf_op jit(solution)/shard_map/reduce_scatter | solution.py:23
  26.5 98.1 %copy-start = (f32[80,1536]{1,0:T(8,128)S(1)}, f32[80,1536]{1,0:T(8,128)}, u32[]{:S(2)}) copy-start(f32[80,1536]{1,0:T(8,128)} %param.9) | copy-start | bytes 1474564
  26.5 171.6 %all-gather.2.cloned.1.call-start = ((), (), s32[]{:S(2)}) async-start(), calls=%async_computation.2 | async-start | bytes 8355840 | tf_op jit(solution)/shard_map/all_gather | solution.py:26
Sparse Core Ops, SparseCore 0:
  26.6 97.8 reduce-scatter.1
  127.4 70.6 all-gather.1
where the time goes:
time: 212 us
  waiting for transfers between devices  170 us (80%)
  other arithmetic  21.1 us (10%)
  between operations  14 us (7%)
  local copies, waits for them, and re-layouts  7.1 us (3%)
    reduce_scatter x1, waiting for transfers between devices, local(): summed = lax.psum_scatter(stepped[0], 'dp', scatter_dimension=0, tiled=True)  98 us
    all_gather x1, waiting for transfers between devices, local(): fresh_weights = lax.all_gather(slow_synced, 'dp', axis=0, tiled=True)  71.6 us
    squeeze x1, other arithmetic, local(): summed = lax.psum_scatter(stepped[0], 'dp', scatter_dimension=0, tiled=True)  19.3 us
    unnamed x3, local copies, waits for them, and re-layouts  7.1 us
  transfers between devices with their start and end apart: 2, of which 2 were waited for; matrix products, arithmetic and copies ran while one was open for 0% of the time, Pallas kernels for 0%

commit v1 on v0

v1 whole, which is shorter than its diff:
```python
import functools
import heapq

import jax
import jax.numpy as jnp
from jax import lax
from jax.experimental import pallas as pl
from jax.experimental.pallas import tpu as pltpu
from jax.sharding import PartitionSpec as P

beta_first = 0.9
beta_second = 0.999
learning_rate = 0.01
weight_decay = 0.05
epsilon = 1e-08
blend_rate = 0.5
first_bias = 1.0 - 0.9**5
second_bias = 1.0 - 0.999**5


def plan(n, chunks):
    bits = n.bit_length() - 1
    inner = (bits - 1) // 2
    near = list(range(1, 1 + inner))
    far = list(range(1 + inner, bits))
    usual = [0] + near + far
    other = [0] + far[:1] + near + far[1:]
    orders = [other if k % 4 == 1 else usual for k in range(chunks)]
    link = {b: 0 if b == 0 else 1 if b in near else 2 for b in range(bits)}
    rate = {0: 6.0, 1: 1.0, 2: 1.0}
    free = {0: 0.0, 1: 0.0, 2: 0.0}
    events, arrivals = [], []

    def start(now, k, s):
        step = s if s < bits else 2 * bits - 1 - s
        b = orders[k][step]
        size = 64.0 / chunks / 2 ** (step + 1)
        begin = max(now, free[link[b]])
        free[link[b]] = begin + size / rate[link[b]]
        heapq.heappush(events, (free[link[b]] + 1.5, k, s))

    for k in range(chunks):
        start(0.0, k, 0)
    while events:
        now, k, s = heapq.heappop(events)
        arrivals.append((k, s))
        if s + 1 < 2 * bits:
            start(now + 0.3, k, s + 1)
    return orders, arrivals


def sync_kernel(n, chunks, orders, arrivals, x_ref, slow_ref, fresh_ref, synced_ref, *scratch):
    bits = n.bit_length() - 1
    parts = scratch[:bits]
    landed = scratch[bits : 2 * bits]
    gathered, send_sem, recv_sem = scratch[2 * bits :]
    width = x_ref.shape[-1] // chunks
    me = lax.axis_index("dp")
    bit = [(me // 2**b) % 2 for b in range(bits)]
    partner = [me + 2**b - 2 * 2**b * bit[b] for b in range(bits)]

    barrier = pltpu.get_barrier_semaphore()
    for b in range(bits):
        pl.semaphore_signal(barrier, inc=1, device_id={"dp": partner[b]}, device_id_type=pl.DeviceIdType.MESH)
    pl.semaphore_wait(barrier, bits)

    def columns(k):
        return pl.ds(k * width, width)

    def offset(k, depth):
        at = 0
        for s in range(1, depth):
            at = at + bit[orders[k][s]] * (n >> (s + 1))
        return at

    def place(k, block):
        at = 0
        for s in range(1, bits):
            at += ((block >> (orders[k][s] - 1)) & 1) * (n >> (s + 1))
        return at

    def copy(k, s):
        if s < bits:
            b = orders[k][s]
            if s == 0:
                src = x_ref.at[:, 1 - bit[0], :, columns(k)]
            else:
                half = n >> (s + 1)
                src = parts[s - 1].at[k, pl.ds((1 - bit[b]) * half, half)]
            dst = landed[s].at[k]
        else:
            step = 2 * bits - 1 - s
            b = orders[k][step]
            if step == 0:
                src = dst = fresh_ref.at[:, bit[0], :, columns(k)]
            else:
                src = dst = gathered.at[k, pl.ds(offset(k, step + 1), n >> (step + 1))]
        return pltpu.make_async_remote_copy(
            src_ref=src,
            dst_ref=dst,
            send_sem=send_sem.at[k, s],
            recv_sem=recv_sem.at[k, s],
            device_id={"dp": partner[b]},
            device_id_type=pl.DeviceIdType.MESH,
        )

    for k in range(chunks):
        copy(k, 0).start()

    for k, s in arrivals:
        copy(k, s).wait_recv()
        if s == 0:
            for block in range(n // 2):
                parts[0][k, place(k, block)] = x_ref[block, bit[0], :, columns(k)] + landed[0][k, block]
        elif s < bits:
            half = n >> (s + 1)
            mine = bit[orders[k][s]] * half
            for block in range(half):
                parts[s][k, block] = parts[s - 1][k, mine + block] + landed[s][k, block]
        if s == bits - 1:
            average = parts[s][k, 0] / n
            slow = slow_ref[:, columns(k)]
            synced = slow + blend_rate * (average - slow)
            synced_ref[:, columns(k)] = synced
            gathered[k, offset(k, bits)] = synced
        if s == 2 * bits - 2:
            for block in range(n // 2):
                fresh_ref[block, bit[0], :, columns(k)] = gathered[k, place(k, block)]
        if s + 1 < 2 * bits:
            copy(k, s + 1).start()

    for k in range(chunks):
        for s in range(2 * bits):
            copy(k, s).wait_send()


def synchronise(n, stepped, slow_weights):
    rows, cols = stepped.shape
    own = rows // n
    width = 256 if cols % 256 == 0 else 128
    chunks = cols // width
    bits = n.bit_length() - 1
    orders, arrivals = plan(n, chunks)
    f32 = jnp.float32
    fresh, synced = pl.pallas_call(
        functools.partial(sync_kernel, n, chunks, orders, arrivals),
        out_shape=(
            jax.ShapeDtypeStruct((n // 2, 2, own, cols), f32),
            jax.ShapeDtypeStruct((own, cols), f32),
        ),
        in_specs=[pl.BlockSpec(memory_space=pltpu.VMEM)] * 2,
        out_specs=[pl.BlockSpec(memory_space=pltpu.VMEM)] * 2,
        scratch_shapes=[
            *[pltpu.VMEM((chunks, n >> (s + 1), own, width), f32) for s in range(bits)],
            *[pltpu.VMEM((chunks, n >> (s + 1), own, width), f32) for s in range(bits)],
            pltpu.VMEM((chunks, n // 2, own, width), f32),
            pltpu.SemaphoreType.DMA((chunks, 2 * bits)),
            pltpu.SemaphoreType.DMA((chunks, 2 * bits)),
        ],
        compiler_params=pltpu.CompilerParams(
            collective_id=0, has_side_effects=True, vmem_limit_bytes=56 * 2**20
        ),
        name="sync",
    )(stepped.reshape(n // 2, 2, own, cols), slow_weights)
    return fresh.reshape(rows, cols), synced


def local(n, fast_weights, gradient, first_moment, second_moment, slow_weights):
    grad_value = gradient.astype(jnp.float32)
    new_first = beta_first * first_moment + (1.0 - beta_first) * grad_value
    new_second = beta_second * second_moment + (1.0 - beta_second) * grad_value * grad_value
    direction = new_first / first_bias / (jnp.sqrt(new_second / second_bias) + epsilon)
    stepped = fast_weights - learning_rate * (direction + weight_decay * fast_weights)
    fresh_weights, slow_synced = synchronise(n, stepped[0], slow_weights)
    return (fresh_weights, slow_synced, new_first, new_second)


def solution(mesh):
    return jax.shard_map(
        functools.partial(local, mesh.shape["dp"]),
        mesh=mesh,
        in_specs=(
            P("dp", None, "shard"),
            P("dp", None, "shard"),
            P("dp", None, "shard"),
            P("dp", None, "shard"),
            P("dp", "shard"),
        ),
        out_specs=(
            P(None, "shard"),
            P("dp", "shard"),
            P("dp", None, "shard"),
            P("dp", None, "shard"),
        ),
        check_vma=False,
    )
```

time: 212 us -> 141 us (0.67)
  waiting for transfers between devices: 170 us -> 0 us
  Pallas kernels: 0 us -> 112 us
  between operations: 14 us -> 0.65 us
    pallas_call x0 -> x1, Pallas kernels: none -> 112 us  [synchronise(): pl.pallas_call(functools.partial(sync_kernel, n, chunks, orders, arrivals...]
    reduce_scatter x1 -> x0, waiting for transfers between devices: 98 us -> none  [local(): summed = lax.psum_scatter(stepped[0], 'dp', scatter_dimension=0, tiled=True)]
    all_gather x1 -> x0, waiting for transfers between devices: 71.6 us -> none  [local(): fresh_weights = lax.all_gather(slow_synced, 'dp', axis=0, tiled=True)]
    squeeze x1 -> x0, other arithmetic: 19.3 us -> none  [local(): summed = lax.psum_scatter(stepped[0], 'dp', scatter_dimension=0, tiled=True)]
    sub x0 -> x1, other arithmetic: none -> 19.3 us  [local(): fast_weights - learning_rate * (direction + weight_decay * fast_weights)]
    unnamed x3 -> x4, local copies, waits for them, and re-layouts: 7.1 us -> 7.94 us
  transfers between devices with their start and end apart: 2 -> 0, of which waited for: 2 -> 0; matrix products, arithmetic and copies ran while one was open for 0% -> 0% of each run, Pallas kernels for 0% -> 0%
where the time goes in v1:
time: 141 us; the launch traced here: 140 us
  Pallas kernels  112 us (79%)
  other arithmetic  19.3 us (14%)
  local copies, waits for them, and re-layouts  7.94 us (6%)
    pallas_call x1, Pallas kernels, synchronise(): pl.pallas_call(functools.partial(sync_kernel, n, chunks, orders, arrivals...  112 us
    sub x1, other arithmetic, local(): fast_weights - learning_rate * (direction + weight_decay * fast_weights)  19.3 us
    unnamed x4, local copies, waits for them, and re-layouts  7.94 us

profile of v1, /device:TPU:0, one launch (start us, length us, event | category | flops | bytes accessed | tf_op | source)
XLA Modules:
  0.0 140.3 jit_solution(7322432827074476754)
XLA Ops:
  0.6 19.3 %multiply_subtract_fusion = (f32[1,1280,1536]{2,1,0:T(8,128)}, f32[1,1280,1536]{2,1,0:T(8,128)}, f32[1,1280,1536]{2,1,0:T(8,128)}) fusion(f32[1,1280,1536]{2,1,0:T(8,128)} %param.5, bf16[1,1280,1536]{2,1,0:T(8,128)(2,1)} %param.6, f32[1,1280,1536]{2,1,0:T(8,128)} %param.7, f32[1,1280,1536]{2,1,0:T(8,128)} %param.8), kind=kLoop, calls=%fused_computation.4 | loop fusion | flops 31457280 | bytes 51118080 | tf_op jit(solution)/shard_map/sub | solution.py:173
  19.9 112.5 %sync.1 = (f32[8,2,80,1536]{3,2,1,0:T(8,128)}, f32[80,1536]{1,0:T(8,128)}) custom-call(f32[8,2,80,1536]{3,2,1,0:T(8,128)} %bitcast.2, f32[80,1536]{1,0:T(8,128)} %slow_ref.1), custom_call_target="tpu_custom_call" | custom-call | tf_op jit(solution)/shard_map/sync/pallas_call | solution.py:145
  132.4 0.0 copy-start
  132.4 7.2 %copy.11 = f32[1280,1536]{1,0:T(8,128)} copy(f32[1280,1536]{1,0:T(8,128)} %bitcast.3) | data formatting | bytes 15728640
  139.5 0.0 copy-done
  139.5 0.8 copy.12
Async XLA Ops:
  132.4 7.2 %copy-start = (f32[80,1536]{1,0:T(8,128)S(1)}, f32[80,1536]{1,0:T(8,128)}, u32[]{:S(2)}) copy-start(f32[80,1536]{1,0:T(8,128)} %get-tuple-element.16) | copy-start | bytes 1474564

commit v2 on v0

v2 whole, which is shorter than its diff:
```python
import functools
import heapq

import jax
import jax.numpy as jnp
from jax import lax
from jax.experimental import pallas as pl
from jax.experimental.pallas import tpu as pltpu
from jax.sharding import PartitionSpec as P

beta_first = 0.9
beta_second = 0.999
learning_rate = 0.01
weight_decay = 0.05
epsilon = 1e-08
blend_rate = 0.5
first_bias = 1.0 - 0.9**5
second_bias = 1.0 - 0.999**5


def grid_of(n):
    chips = n // 2
    fast = 2 ** ((chips.bit_length() - 1) // 2)
    return chips // fast, fast


def plan(n, chunks):
    slow, fast = grid_of(n)
    orders = [((0, slow), (1, fast)) if (k + 1) * 5 // 12 > k * 5 // 12 else ((1, fast), (0, slow)) for k in range(chunks)]
    free, queued, events, arrivals = {}, {}, [], []

    def send(now, link, units):
        free[link] = max(now, free.get(link, 0.0)) + units * (0.15 if link == "core" else 0.9)
        return free[link]

    def line_of(k, stage):
        at = stage - 1 if stage < 3 else 4 - stage
        return orders[k][at] + (orders[k][1][1] if at == 0 else 1,)

    def start(now, k, stage, tick):
        if stage in (0, 5):
            done = send(now, "core", n // 2)
        else:
            axis, length, units = line_of(k, stage)
            if stage < 3:
                if tick == 0:
                    queued[k, stage] = [send(now, (axis, 0), units) for _ in range(length - 1)]
                ends = [queued[k, stage][tick]] + [send(now, (axis, i), units) for i in range(1, tick + 1)]
            else:
                ends = [send(now, (axis, i), units) for i in range(tick, length - 1)]
            done = max(ends)
        heapq.heappush(events, (done + 1.8, k, stage, tick))

    for k in range(chunks):
        start(0.3 * k, k, 0, 0)
    while events:
        now, k, stage, tick = heapq.heappop(events)
        arrivals.append((k, stage, tick))
        last = stage in (0, 5) or tick == line_of(k, stage)[1] - 2
        if not last:
            start(now + 0.1, k, stage, tick + 1)
        elif stage < 5:
            start(now + 0.2, k, stage + 1, 0)
    return orders, arrivals


def sync_kernel(n, chunks, orders, arrivals, x_hbm, slow_ref, fresh_ref, synced_ref, *scratch):
    x_ref, load_sem, send_sem, recv_sem = scratch[:4]
    buffers = [scratch[4 + 6 * k : 10 + 6 * k] for k in range(chunks)]
    width = x_ref.shape[-1] // chunks
    slow, fast = grid_of(n)
    me = lax.axis_index("dp")
    core = me % 2
    places = (me // (2 * fast), (me // 2) % fast)
    strides = (2 * fast, 2)
    other = me + 1 - 2 * core

    def columns(k):
        return pl.ds(k * width, width)

    def load(k):
        return pltpu.make_async_copy(x_hbm.at[:, :, :, columns(k)], x_ref.at[:, :, :, columns(k)], load_sem.at[k])

    for k in range(chunks):
        load(k).start()

    barrier = pltpu.get_barrier_semaphore()

    def greet(device):
        pl.semaphore_signal(barrier, inc=1, device_id={"dp": device}, device_id_type=pl.DeviceIdType.MESH)

    greet(other)
    peers = 1
    for axis, length in enumerate((slow, fast)):
        below, above = places[axis] > 0, places[axis] < length - 1
        pl.when(below)(functools.partial(greet, me - strides[axis]))
        pl.when(above)(functools.partial(greet, me + strides[axis]))
        peers = peers + jnp.where(below, 1, 0) + jnp.where(above, 1, 0)
    pl.semaphore_wait(barrier, peers)

    def copy(k, stage, tick, way, src, dst, device):
        return pltpu.make_async_remote_copy(
            src_ref=src,
            dst_ref=dst,
            send_sem=send_sem.at[k, stage, tick, way],
            recv_sem=recv_sem.at[k, stage, tick, way],
            device_id={"dp": device},
            device_id_type=pl.DeviceIdType.MESH,
        )

    def core_copy(k, stage):
        if stage == 0:
            src, dst = x_ref.at[:, 1 - core, :, columns(k)], buffers[k][0]
        else:
            src = dst = fresh_ref.at[:, core, :, columns(k)]
        return copy(k, stage, 0, 0, src, dst, other)

    class Line:
        def __init__(self, k, stage):
            at = stage - 1 if stage < 3 else 4 - stage
            self.k, self.stage = k, stage
            axis, self.length = orders[k][at]
            self.place = places[axis]
            self.units = orders[k][1][1] if at == 0 else 1
            self.step = strides[axis]
            landed0, sums, landed1, middle, landed2, gathered = buffers[k]
            self.source = sums if at == 0 else middle
            self.landed = landed1 if at == 0 else landed2
            self.gathered = gathered
            self.base = 0 if at == 0 else places[orders[k][0][0]] * orders[k][1][1]

        def far(self, way):
            return self.place if way == 0 else self.length - 1 - self.place

        def real(self, way, block):
            return block if way == 0 else self.length - 1 - block

        def block(self, way, block):
            return pl.ds(self.real(way, block) * self.units, self.units)

        def held(self, way, block):
            return self.gathered.at[pl.ds(self.base + self.real(way, block) * self.units, self.units)]

        def next(self, way):
            return me + self.step if way == 0 else me - self.step

        def copy(self, tick, way, src, dst):
            return copy(self.k, self.stage, tick, way, src, dst, self.next(way))

        def arrived(self, tick, way):
            if self.stage < 3:
                ref = self.landed.at[way, tick]
            else:
                ref = self.held(way, self.far(way) - 1 - tick)
            self.copy(tick, way, ref, ref).wait_recv()

        def begin(self):
            for way in (0, 1):
                far = self.far(way)
                if self.stage < 3:

                    @pl.when(far == 0)
                    def _():
                        for tick in range(self.length - 1):
                            src = self.source.at[self.block(way, self.length - 1 - tick)]
                            self.copy(tick, way, src, self.landed.at[way, tick]).start()
                else:

                    @pl.when(far < self.length - 1)
                    def _():
                        own = self.held(way, far)
                        self.copy(0, way, own, own).start()

        def reduce(self, tick, out):
            last = self.length - 2
            if tick < last:
                for way in (0, 1):
                    far = self.far(way)

                    @pl.when((far >= 1) & (far <= tick + 1))
                    def _():
                        self.arrived(tick, way)
                        here = self.landed.at[way, tick]
                        here[...] += self.source[self.block(way, last - tick + far)]
                        self.copy(tick + 1, way, here, self.landed.at[way, tick + 1]).start()
                return
            mine = pl.ds(self.place * self.units, self.units)

            @pl.when(self.place == 0)
            def _():
                self.arrived(last, 1)
                out[...] = self.source[mine] + self.landed[1, last]

            @pl.when(self.place == self.length - 1)
            def _():
                self.arrived(last, 0)
                out[...] = self.source[mine] + self.landed[0, last]

            if self.length > 2:

                @pl.when((self.place > 0) & (self.place < self.length - 1))
                def _():
                    self.arrived(last, 0)
                    self.arrived(last, 1)
                    out[...] = self.source[mine] + self.landed[0, last] + self.landed[1, last]

        def gather(self, tick):
            for way in (0, 1):
                far = self.far(way)

                @pl.when(far >= 1 + tick)
                def _():
                    self.arrived(tick, way)
                    if tick < self.length - 2:

                        @pl.when(far < self.length - 1)
                        def _():
                            got = self.held(way, far - 1 - tick)
                            self.copy(tick + 1, way, got, got).start()

        def sent(self):
            for way in (0, 1):
                far = self.far(way)
                for tick in range(self.length - 1):
                    if self.stage < 3:
                        ref, did = self.landed.at[way, tick], far <= tick
                    else:
                        ref, did = self.held(way, far - tick), far >= tick

                    @pl.when(did & (far < self.length - 1))
                    def _():
                        self.copy(tick, way, ref, ref).wait_send()

    def position(k, pair):
        where = (pair // fast, pair % fast)
        (first, _), (second, length) = orders[k]
        return where[first] * length + where[second]

    for k in range(chunks):
        load(k).wait()
        core_copy(k, 0).start()

    for k, stage, tick in arrivals:
        landed0, sums, landed1, middle, landed2, gathered = buffers[k]
        if stage == 0:
            core_copy(k, 0).wait_recv()
            for pair in range(n // 2):
                sums[position(k, pair)] = x_ref[pair, core, :, columns(k)] + landed0[pair]
            Line(k, 1).begin()
        elif stage == 5:
            core_copy(k, 5).wait_recv()
        else:
            line = Line(k, stage)
            last = tick == line.length - 2
            if stage == 1:
                line.reduce(tick, middle)
            elif stage == 2:
                own = gathered.at[pl.ds(line.base + line.place, 1)]
                line.reduce(tick, own)
                if last:
                    average = own[0] / n
                    slow_part = slow_ref[:, columns(k)]
                    synced = slow_part + blend_rate * (average - slow_part)
                    synced_ref[:, columns(k)] = synced
                    own[0] = synced
            else:
                line.gather(tick)
            if last and stage < 4:
                Line(k, stage + 1).begin()
            elif last:
                for pair in range(n // 2):
                    fresh_ref[pair, core, :, columns(k)] = gathered[position(k, pair)]
                core_copy(k, 5).start()

    for k in range(chunks):
        core_copy(k, 0).wait_send()
        for stage in (1, 2, 3, 4):
            Line(k, stage).sent()
        core_copy(k, 5).wait_send()


def synchronise(n, stepped, slow_weights):
    rows, cols = stepped.shape
    own = rows // n
    width = 128
    chunks = cols // width
    orders, arrivals = plan(n, chunks)
    slow, fast = grid_of(n)
    ticks = max(slow, fast) - 1
    f32 = jnp.float32
    buffers = []
    for (_, first), (_, second) in orders:
        buffers += [
            pltpu.VMEM((n // 2, own, width), f32),
            pltpu.VMEM((n // 2, own, width), f32),
            pltpu.VMEM((2, first - 1, second, own, width), f32),
            pltpu.VMEM((second, own, width), f32),
            pltpu.VMEM((2, second - 1, 1, own, width), f32),
            pltpu.VMEM((n // 2, own, width), f32),
        ]
    fresh, synced = pl.pallas_call(
        functools.partial(sync_kernel, n, chunks, orders, arrivals),
        out_shape=(
            pltpu.VMEM((n // 2, 2, own, cols), f32),
            jax.ShapeDtypeStruct((own, cols), f32),
        ),
        in_specs=[pl.BlockSpec(memory_space=pl.ANY), pl.BlockSpec(memory_space=pltpu.VMEM)],
        out_specs=[pl.BlockSpec(memory_space=pltpu.VMEM)] * 2,
        scratch_shapes=[
            pltpu.VMEM((n // 2, 2, own, cols), f32),
            pltpu.SemaphoreType.DMA((chunks,)),
            pltpu.SemaphoreType.DMA((chunks, 6, ticks, 2)),
            pltpu.SemaphoreType.DMA((chunks, 6, ticks, 2)),
            *buffers,
        ],
        compiler_params=pltpu.CompilerParams(
            collective_id=0, has_side_effects=True, vmem_limit_bytes=48 * 2**20
        ),
        name="sync",
    )(stepped.reshape(n // 2, 2, own, cols), slow_weights)
    return fresh.reshape(rows, cols), synced


def local(n, fast_weights, gradient, first_moment, second_moment, slow_weights):
    grad_value = gradient.astype(jnp.float32)
    new_first = beta_first * first_moment + (1.0 - beta_first) * grad_value
    new_second = beta_second * second_moment + (1.0 - beta_second) * grad_value * grad_value
    direction = new_first / first_bias / (jnp.sqrt(new_second / second_bias) + epsilon)
    stepped = fast_weights - learning_rate * (direction + weight_decay * fast_weights)
    fresh_weights, slow_synced = synchronise(n, stepped[0], slow_weights)
    return (fresh_weights, slow_synced, new_first, new_second)


def solution(mesh):
    return jax.shard_map(
        functools.partial(local, mesh.shape["dp"]),
        mesh=mesh,
        in_specs=(
            P("dp", None, "shard"),
            P("dp", None, "shard"),
            P("dp", None, "shard"),
            P("dp", None, "shard"),
            P("dp", "shard"),
        ),
        out_specs=(
            P(None, "shard"),
            P("dp", "shard"),
            P("dp", None, "shard"),
            P("dp", None, "shard"),
        ),
        check_vma=False,
    )
```

time: 212 us -> 143 us (0.67)
  waiting for transfers between devices: 170 us -> 0 us
  Pallas kernels: 0 us -> 119 us
  between operations: 14 us -> 0.65 us
  local copies, waits for them, and re-layouts: 7.1 us -> 4.01 us
    pallas_call x0 -> x1, Pallas kernels: none -> 119 us  [synchronise(): pl.pallas_call(functools.partial(sync_kernel, n, chunks, orders, arrivals...]
    reduce_scatter x1 -> x0, waiting for transfers between devices: 98 us -> none  [local(): summed = lax.psum_scatter(stepped[0], 'dp', scatter_dimension=0, tiled=True)]
    all_gather x1 -> x0, waiting for transfers between devices: 71.6 us -> none  [local(): fresh_weights = lax.all_gather(slow_synced, 'dp', axis=0, tiled=True)]
    squeeze x1 -> x0, other arithmetic: 19.3 us -> none  [local(): summed = lax.psum_scatter(stepped[0], 'dp', scatter_dimension=0, tiled=True)]
    sub x0 -> x1, other arithmetic: none -> 19.3 us  [local(): fast_weights - learning_rate * (direction + weight_decay * fast_weights)]
    unnamed x3 -> x4, local copies, waits for them, and re-layouts: 7.1 us -> 4.01 us
  transfers between devices with their start and end apart: 2 -> 0, of which waited for: 2 -> 0; matrix products, arithmetic and copies ran while one was open for 0% -> 0% of each run, Pallas kernels for 0% -> 0%
where the time goes in v2:
time: 143 us; the launch traced here: 142 us
  Pallas kernels  119 us (83%)
  other arithmetic  19.3 us (13%)
  local copies, waits for them, and re-layouts  4.01 us (3%)
    pallas_call x1, Pallas kernels, synchronise(): pl.pallas_call(functools.partial(sync_kernel, n, chunks, orders, arrivals...  119 us
    sub x1, other arithmetic, local(): fast_weights - learning_rate * (direction + weight_decay * fast_weights)  19.3 us
    unnamed x4, local copies, waits for them, and re-layouts  4.01 us

profile of v2, /device:TPU:0, one launch (start us, length us, event | category | flops | bytes accessed | tf_op | source)
XLA Modules:
  0.0 142.5 jit_solution(8762413258534922025)
XLA Ops:
  0.6 19.3 %multiply_subtract_fusion = (f32[1,1280,1536]{2,1,0:T(8,128)}, f32[1,1280,1536]{2,1,0:T(8,128)}, f32[1,1280,1536]{2,1,0:T(8,128)}) fusion(f32[1,1280,1536]{2,1,0:T(8,128)} %param.5, bf16[1,1280,1536]{2,1,0:T(8,128)(2,1)} %param.6, f32[1,1280,1536]{2,1,0:T(8,128)} %param.7, f32[1,1280,1536]{2,1,0:T(8,128)} %param.8), kind=kLoop, calls=%fused_computation.4 | loop fusion | flops 31457280 | bytes 51118080 | tf_op jit(solution)/shard_map/sub | solution.py:329
  19.9 118.6 %sync.1 = (f32[8,2,80,1536]{3,2,1,0:T(8,128)S(1)}, f32[80,1536]{1,0:T(8,128)}) custom-call(f32[8,2,80,1536]{3,2,1,0:T(8,128)} %bitcast.3, f32[80,1536]{1,0:T(8,128)} %slow_ref.1), custom_call_target="tpu_custom_call" | custom-call | tf_op jit(solution)/shard_map/sync/pallas_call | solution.py:301
  138.5 0.0 copy-start
  138.5 3.2 %copy.11 = f32[1280,1536]{1,0:T(8,128)} copy(f32[1280,1536]{1,0:T(8,128)S(1)} %bitcast.2) | data formatting | bytes 15728640
  141.7 0.0 copy-done
  141.7 0.8 copy.12
Async XLA Ops:
  138.5 3.2 %copy-start = (f32[80,1536]{1,0:T(8,128)S(1)}, f32[80,1536]{1,0:T(8,128)}, u32[]{:S(2)}) copy-start(f32[80,1536]{1,0:T(8,128)} %get-tuple-element.20) | copy-start | bytes 1474564

commit v3 on v2

--- a/solution.py
+++ b/solution.py
@@ -26,7 +26,7 @@
 
 def plan(n, chunks):
     slow, fast = grid_of(n)
-    orders = [((0, slow), (1, fast)) if (k + 1) * 5 // 12 > k * 5 // 12 else ((1, fast), (0, slow)) for k in range(chunks)]
+    orders = [((1, fast), (0, slow))] * chunks
     free, queued, events, arrivals = {}, {}, [], []
 
     def send(now, link, units):
@@ -52,11 +52,11 @@
         heapq.heappush(events, (done + 1.8, k, stage, tick))
 
     for k in range(chunks):
-        start(0.3 * k, k, 0, 0)
+        heapq.heappush(events, (2.0 + 1.0 * k, k, -1, 0))
     while events:
         now, k, stage, tick = heapq.heappop(events)
         arrivals.append((k, stage, tick))
-        last = stage in (0, 5) or tick == line_of(k, stage)[1] - 2
+        last = stage in (-1, 0, 5) or tick == line_of(k, stage)[1] - 2
         if not last:
             start(now + 0.1, k, stage, tick + 1)
         elif stage < 5:
@@ -64,9 +64,9 @@
     return orders, arrivals
 
 
-def sync_kernel(n, chunks, orders, arrivals, x_hbm, slow_ref, fresh_ref, synced_ref, *scratch):
-    x_ref, load_sem, send_sem, recv_sem = scratch[:4]
-    buffers = [scratch[4 + 6 * k : 10 + 6 * k] for k in range(chunks)]
+def sync_kernel(n, chunks, orders, arrivals, fast_hbm, grad_hbm, first_hbm, second_hbm, slow_ref, fresh_ref, synced_ref, first_ref, second_ref, *scratch):
+    x_ref, grad_ref, load_sem, send_sem, recv_sem = scratch[:5]
+    buffers = [scratch[5 + 6 * k : 11 + 6 * k] for k in range(chunks)]
     width = x_ref.shape[-1] // chunks
     slow, fast = grid_of(n)
     me = lax.axis_index("dp")
@@ -78,11 +78,30 @@
     def columns(k):
         return pl.ds(k * width, width)
 
-    def load(k):
-        return pltpu.make_async_copy(x_hbm.at[:, :, :, columns(k)], x_ref.at[:, :, :, columns(k)], load_sem.at[k])
+    pairs = ((grad_hbm, grad_ref), (first_hbm, first_ref), (second_hbm, second_ref), (fast_hbm, x_ref))
+
+    def loads(k):
+        return [
+            pltpu.make_async_copy(src.at[:, :, :, columns(k)], dst.at[:, :, :, columns(k)], load_sem.at[k, i])
+            for i, (src, dst) in enumerate(pairs)
+        ]
+
+    def adam(k):
+        @pl.loop(0, n)
+        def _(block):
+            at = (block // 2, block % 2, slice(None), columns(k))
+            grad_value = grad_ref[at].astype(jnp.float32)
+            new_first = beta_first * first_ref[at] + (1.0 - beta_first) * grad_value
+            new_second = beta_second * second_ref[at] + (1.0 - beta_second) * grad_value * grad_value
+            first_ref[at] = new_first
+            second_ref[at] = new_second
+            direction = new_first / first_bias / (jnp.sqrt(new_second / second_bias) + epsilon)
+            weights = x_ref[at]
+            x_ref[at] = weights - learning_rate * (direction + weight_decay * weights)
 
     for k in range(chunks):
-        load(k).start()
+        for load in loads(k):
+            load.start()
 
     barrier = pltpu.get_barrier_semaphore()
 
@@ -236,13 +255,14 @@
         (first, _), (second, length) = orders[k]
         return where[first] * length + where[second]
 
-    for k in range(chunks):
-        load(k).wait()
-        core_copy(k, 0).start()
-
     for k, stage, tick in arrivals:
         landed0, sums, landed1, middle, landed2, gathered = buffers[k]
-        if stage == 0:
+        if stage == -1:
+            for load in loads(k):
+                load.wait()
+            adam(k)
+            core_copy(k, 0).start()
+        elif stage == 0:
             core_copy(k, 0).wait_recv()
             for pair in range(n // 2):
                 sums[position(k, pair)] = x_ref[pair, core, :, columns(k)] + landed0[pair]
@@ -279,8 +299,8 @@
         core_copy(k, 5).wait_send()
 
 
-def synchronise(n, stepped, slow_weights):
-    rows, cols = stepped.shape
+def synchronise(n, fast_weights, gradient, first_moment, second_moment, slow_weights):
+    _, rows, cols = fast_weights.shape
     own = rows // n
     width = 128
     chunks = cols // width
@@ -298,42 +318,37 @@
             pltpu.VMEM((2, second - 1, 1, own, width), f32),
             pltpu.VMEM((n // 2, own, width), f32),
         ]
-    fresh, synced = pl.pallas_call(
+    blocks = (n // 2, 2, own, cols)
+    fresh, synced, new_first, new_second = pl.pallas_call(
         functools.partial(sync_kernel, n, chunks, orders, arrivals),
         out_shape=(
-            pltpu.VMEM((n // 2, 2, own, cols), f32),
+            pltpu.VMEM(blocks, f32),
             jax.ShapeDtypeStruct((own, cols), f32),
+            pltpu.VMEM(blocks, f32),
+            pltpu.VMEM(blocks, f32),
         ),
-        in_specs=[pl.BlockSpec(memory_space=pl.ANY), pl.BlockSpec(memory_space=pltpu.VMEM)],
-        out_specs=[pl.BlockSpec(memory_space=pltpu.VMEM)] * 2,
+        in_specs=[pl.BlockSpec(memory_space=pl.ANY)] * 4 + [pl.BlockSpec(memory_space=pltpu.VMEM)],
+        out_specs=[pl.BlockSpec(memory_space=pltpu.VMEM)] * 4,
         scratch_shapes=[
-            pltpu.VMEM((n // 2, 2, own, cols), f32),
-            pltpu.SemaphoreType.DMA((chunks,)),
+            pltpu.VMEM(blocks, f32),
+            pltpu.VMEM(blocks, jnp.bfloat16),
+            pltpu.SemaphoreType.DMA((chunks, 4)),
             pltpu.SemaphoreType.DMA((chunks, 6, ticks, 2)),
             pltpu.SemaphoreType.DMA((chunks, 6, ticks, 2)),
             *buffers,
         ],
         compiler_params=pltpu.CompilerParams(
-            collective_id=0, has_side_effects=True, vmem_limit_bytes=48 * 2**20
+            collective_id=0, has_side_effects=True, vmem_limit_bytes=36 * 2**20
         ),
         name="sync",
-    )(stepped.reshape(n // 2, 2, own, cols), slow_weights)
-    return fresh.reshape(rows, cols), synced
-
-
-def local(n, fast_weights, gradient, first_moment, second_moment, slow_weights):
-    grad_value = gradient.astype(jnp.float32)
-    new_first = beta_first * first_moment + (1.0 - beta_first) * grad_value
-    new_second = beta_second * second_moment + (1.0 - beta_second) * grad_value * grad_value
-    direction = new_first / first_bias / (jnp.sqrt(new_second / second_bias) + epsilon)
-    stepped = fast_weights - learning_rate * (direction + weight_decay * fast_weights)
-    fresh_weights, slow_synced = synchronise(n, stepped[0], slow_weights)
-    return (fresh_weights, slow_synced, new_first, new_second)
+    )(*(array.reshape(blocks) for array in (fast_weights, gradient, first_moment, second_moment)), slow_weights)
+    whole = fast_weights.shape
+    return fresh.reshape(rows, cols), synced, new_first.reshape(whole), new_second.reshape(whole)
 
 
 def solution(mesh):
     return jax.shard_map(
-        functools.partial(local, mesh.shape["dp"]),
+        functools.partial(synchronise, mesh.shape["dp"]),
         mesh=mesh,
         in_specs=(
             P("dp", None, "shard"),

time: 143 us -> 115 us (0.80)
  other arithmetic: 19.3 us -> 0 us
  Pallas kernels: 119 us -> 104 us
  local copies, waits for them, and re-layouts: 4.01 us -> 10.4 us
    sub x1 -> x0, other arithmetic: 19.3 us -> none  [local(): fast_weights - learning_rate * (direction + weight_decay * fast_weights)]
    pallas_call x1, Pallas kernels: 119 us -> 104 us  [synchronise(): pl.pallas_call(functools.partial(sync_kernel, n, chunks, orders, arrivals...]
    unnamed x4 -> x6, local copies, waits for them, and re-layouts: 4.01 us -> 10.4 us
where the time goes in v3:
time: 115 us
  Pallas kernels  104 us (90%)
  local copies, waits for them, and re-layouts  10.4 us (9%)
    pallas_call x1, Pallas kernels, synchronise(): pl.pallas_call(functools.partial(sync_kernel, n, chunks, orders, arrivals...  104 us
    unnamed x6, local copies, waits for them, and re-layouts  10.4 us

profile of v3, /device:TPU:0, one launch (start us, length us, event | category | flops | bytes accessed | tf_op | source)
XLA Modules:
  0.0 115.1 jit_solution(6104814938450670854)
XLA Ops:
  0.6 104.0 %sync.1 = (f32[8,2,80,1536]{3,2,1,0:T(8,128)S(1)}, f32[80,1536]{1,0:T(8,128)}, f32[8,2,80,1536]{3,2,1,0:T(8,128)S(1)}, f32[8,2,80,1536]{3,2,1,0:T(8,128)S(1)}) custom-call(f32[8,2,80,1536]{3,2,1,0:T(8,128)} %bitcast.10, bf16[8,2,80,1536]{3,2,1,0:T(8,128)(2,1)} %bitcast.13, f32[8,2,80,1536]{3,2,1,0:T(8,128)} %bitcast.11, f32[8,2,80,1536]{3,2,1,0:T(8,128)} %bitcast.12, ...), custom_call_target="tpu_custom_call" | custom-call | tf_op jit(solution)/shard_map/sync/pallas_call | solution.py:322
  104.7 3.2 %copy.13 = f32[1280,1536]{1,0:T(8,128)} copy(f32[1280,1536]{1,0:T(8,128)S(1)} %bitcast.9) | data formatting | bytes 15728640
  107.9 3.2 %copy.14 = f32[1,1280,1536]{2,1,0:T(8,128)} copy(f32[1,1280,1536]{2,1,0:T(8,128)S(1)} %bitcast.8) | data formatting | bytes 15728640
  111.1 0.0 copy-start
  111.1 3.2 %copy.15 = f32[1,1280,1536]{2,1,0:T(8,128)} copy(f32[1,1280,1536]{2,1,0:T(8,128)S(1)} %bitcast.7) | data formatting | bytes 15728640
  114.4 0.0 copy-done
  114.4 0.8 copy.16
Async XLA Ops:
  111.1 3.2 %copy-start = (f32[80,1536]{1,0:T(8,128)S(1)}, f32[80,1536]{1,0:T(8,128)}, u32[]{:S(2)}) copy-start(f32[80,1536]{1,0:T(8,128)} %get-tuple-element.21) | copy-start | bytes 1474564

commit v4 on v3

--- a/solution.py
+++ b/solution.py
@@ -52,7 +52,7 @@
         heapq.heappush(events, (done + 1.8, k, stage, tick))
 
     for k in range(chunks):
-        heapq.heappush(events, (2.0 + 1.0 * k, k, -1, 0))
+        heapq.heappush(events, (2.0 + 2.0 * k, k, -1, 0))
     while events:
         now, k, stage, tick = heapq.heappop(events)
         arrivals.append((k, stage, tick))
@@ -302,7 +302,7 @@
 def synchronise(n, fast_weights, gradient, first_moment, second_moment, slow_weights):
     _, rows, cols = fast_weights.shape
     own = rows // n
-    width = 128
+    width = 256 if cols % 256 == 0 else 128
     chunks = cols // width
     orders, arrivals = plan(n, chunks)
     slow, fast = grid_of(n)

time: 115 us -> 114 us (level)
    pallas_call x1, Pallas kernels: 104 us -> 103 us  [synchronise(): pl.pallas_call(functools.partial(sync_kernel, n, chunks, orders, arrivals...]
where the time goes in v4:
time: 114 us
  Pallas kernels  103 us (90%)
  local copies, waits for them, and re-layouts  10.4 us (9%)
    pallas_call x1, Pallas kernels, synchronise(): pl.pallas_call(functools.partial(sync_kernel, n, chunks, orders, arrivals...  103 us
    unnamed x6, local copies, waits for them, and re-layouts  10.4 us

profile of v4, /device:TPU:0, one launch (start us, length us, event | category | flops | bytes accessed | tf_op | source)
XLA Modules:
  0.0 113.6 jit_solution(16152692356728073870)
XLA Ops:
  0.6 102.5 %sync.1 = (f32[8,2,80,1536]{3,2,1,0:T(8,128)S(1)}, f32[80,1536]{1,0:T(8,128)}, f32[8,2,80,1536]{3,2,1,0:T(8,128)S(1)}, f32[8,2,80,1536]{3,2,1,0:T(8,128)S(1)}) custom-call(f32[8,2,80,1536]{3,2,1,0:T(8,128)} %bitcast.10, bf16[8,2,80,1536]{3,2,1,0:T(8,128)(2,1)} %bitcast.13, f32[8,2,80,1536]{3,2,1,0:T(8,128)} %bitcast.11, f32[8,2,80,1536]{3,2,1,0:T(8,128)} %bitcast.12, ...), custom_call_target="tpu_custom_call" | custom-call | tf_op jit(solution)/shard_map/sync/pallas_call | solution.py:322
  103.1 3.2 %copy.13 = f32[1280,1536]{1,0:T(8,128)} copy(f32[1280,1536]{1,0:T(8,128)S(1)} %bitcast.9) | data formatting | bytes 15728640
  106.4 3.2 %copy.14 = f32[1,1280,1536]{2,1,0:T(8,128)} copy(f32[1,1280,1536]{2,1,0:T(8,128)S(1)} %bitcast.8) | data formatting | bytes 15728640
  109.6 0.0 copy-start
  109.6 3.2 %copy.15 = f32[1,1280,1536]{2,1,0:T(8,128)} copy(f32[1,1280,1536]{2,1,0:T(8,128)S(1)} %bitcast.7) | data formatting | bytes 15728640
  112.8 0.0 copy-done
  112.8 0.8 copy.16
Async XLA Ops:
  109.6 3.2 %copy-start = (f32[80,1536]{1,0:T(8,128)S(1)}, f32[80,1536]{1,0:T(8,128)}, u32[]{:S(2)}) copy-start(f32[80,1536]{1,0:T(8,128)} %get-tuple-element.21) | copy-start | bytes 1474564
